TPU v7x, 128 devices: a whole 4x4x4 slice. The times are simulated.
128 devices in a mesh: var: 16 (over y, z), own: 4 (over x), sub: 2 (over core).
Axes of the slice: x: 4, y: 4, z: 4, core: 2. Of those that a mesh axis runs over, the one named last changes fastest.
Arguments:
- capacity_blocks: bfloat16 [8192, 5, 128, 128], P(('var', 'own', 'sub')), may hold values from -0.0390625 to 0.0390625
- capacity_rows: int32 [8192, 5], P(('var', 'own', 'sub')), may hold values from 0 to 7, all different within a row
- cover_self: bfloat16 [8192, 128, 128], P(('var', 'own', 'sub')), may hold values from -0.5 to 0.5
- cover_prev: bfloat16 [8192, 128, 128], P(('var', 'own', 'sub')), may hold values from -0.5 to 0.5
- scaling: bfloat16 [8192, 128], P(('var', 'own', 'sub')), may hold values from 0.099609375 to 10
Outputs:
- cover_diag: bfloat16 [8192, 128, 128], P(('var', 'own', 'sub'))
- cover_lower: bfloat16 [8192, 128, 128], P(('var', 'own', 'sub'))
- capacity_normal: float32 [1024, 1024], P(('var', 'own', 'sub'))
Inputs may be any that keep to these rules, and one draw needn't show every extreme that they name: `capacity_rows`: each column block names 5 different capacity row blocks, and every capacity row block is named somewhere.
All inputs are finite; a program needn't handle non-finite values.
Results may differ from a plain program's by a relative error of at most 0.0049.
Values may be sent and summed in bfloat16 or wider, within the bound.
A program may use at most 192 MiB of HBM per device.

v0:
```python
import math

import jax
import jax.numpy as jnp
from jax import lax
from jax.sharding import PartitionSpec as P

CAP = 8


def shifted(value, axis, steps):
    count = lax.axis_size(axis)
    initial, last = (max(0, -steps), min(count, count - steps))
    return lax.ppermute(value, axis, [(source, source + steps) for source in range(initial, last)])


def accumulate(partial_value, inputs):
    blocks, row_ids, scale_row = inputs
    scaled = (blocks.astype(jnp.float32) * scale_row.astype(jnp.float32)[:, None, None, :]).astype(
        jnp.bfloat16
    )
    tile_sums = jnp.einsum("kpiv,kqjv->kpqij", scaled, blocks, preferred_element_type=jnp.float32)
    per_block = row_ids.shape[1]
    left_rows = jnp.broadcast_to(
        row_ids[:, :, None], (row_ids.shape[0], per_block, per_block)
    ).reshape(-1)
    right_rows = jnp.broadcast_to(
        row_ids[:, None, :], (row_ids.shape[0], per_block, per_block)
    ).reshape(-1)
    edge_size = blocks.shape[-1]
    partial_value = partial_value.at[left_rows, :, right_rows, :].add(
        tile_sums.reshape(-1, edge_size, edge_size)
    )
    return (partial_value, None)


def body(capacity_blocks, capacity_rows, cover_self, cover_prev, scaling):
    edge_size = capacity_blocks.shape[-1]
    local_blocks = capacity_blocks.shape[0]
    received = shifted((cover_self[-1:], scaling[-1:]), ("var", "own", "sub"), 1)
    group_size = math.gcd(local_blocks, 16)
    turns = local_blocks // group_size
    inputs = (
        capacity_blocks.reshape((turns, group_size) + capacity_blocks.shape[1:]),
        capacity_rows.reshape(turns, group_size, -1),
        scaling.reshape(turns, group_size, -1),
    )
    start = jnp.zeros((CAP, edge_size, CAP, edge_size), jnp.float32)
    result, unused = lax.scan(accumulate, start, inputs)
    full_rows = CAP * edge_size
    flat_sum = result.reshape(full_rows, full_rows)
    capacity_normal = lax.psum_scatter(
        flat_sum, ("var", "own", "sub"), scatter_dimension=0, tiled=True
    )
    self_prev = jnp.concatenate([received[0], cover_self[:-1]], axis=0)
    scale_prev = jnp.concatenate([received[1], scaling[:-1]], axis=0)
    scaled_self = (cover_self.astype(jnp.float32) * scaling.astype(jnp.float32)[:, None, :]).astype(
        jnp.bfloat16
    )
    scaled_prev = (
        cover_prev.astype(jnp.float32) * scale_prev.astype(jnp.float32)[:, None, :]
    ).astype(jnp.bfloat16)
    diag_sum = jnp.einsum(
        "kiv,kjv->kij", scaled_self, cover_self, preferred_element_type=jnp.float32
    )
    diag_sum = diag_sum + jnp.einsum(
        "kiv,kjv->kij", scaled_prev, cover_prev, preferred_element_type=jnp.float32
    )
    lower_sum = jnp.einsum(
        "kiv,kjv->kij", scaled_prev, self_prev, preferred_element_type=jnp.float32
    )
    return (diag_sum.astype(jnp.bfloat16), lower_sum.astype(jnp.bfloat16), capacity_normal)


def solution(mesh):
    placed = (
        P(("var", "own", "sub"), None, None, None),
        P(("var", "own", "sub"), None),
        P(("var", "own", "sub"), None, None),
        P(("var", "own", "sub"), None, None),
        P(("var", "own", "sub"), None),
    )
    return jax.shard_map(
        body,
        mesh=mesh,
        in_specs=placed,
        out_specs=(
            P(("var", "own", "sub"), None, None),
            P(("var", "own", "sub"), None, None),
            P(("var", "own", "sub"), None),
        ),
        check_vma=False,
    )
```

profile of v0, /device:TPU:0, one launch (start us, length us, event | category | flops | bytes accessed | tf_op | source)
XLA Modules:
  0.0 1184.5 jit_solution(7172075704830276296)
XLA Ops:
  7.2 0.0 copy-start.2
  7.2 0.0 reduce-scatter.2.cloned.1.call-start
  7.2 0.8 reshape.110
  8.0 2.5 broadcast_in_dim.8
  10.4 0.0 copy-done.2
  10.4 512.6 %while.10 = (s32[]{:T(128)}, f32[8,128,8,128]{3,1,2,0:T(8,128)}, s32[4,16,5]{1,0,2:T(4,128)S(1)}, bf16[4,16,5,128,128]{4,3,2,1,0:T(8,128)(2,1)}, bf16[4,16,128]{2,1,0:T(8,128)(2,1)S(1)}, /*index=5*/s32[]{:T(128)}) while((s32[]{:T(128)}, f32[8,128,8,128]{3,1,2,0:T(8,128)}, s32[4,16,5]{1,0,2:T(4,128)S(1)}, ...), condition=%wide.region_2.3_spmd, body=%wide.region_0.2_spmd.sunk | while | flops 1688215424 | bytes 162570400 | solution.py:49
  10.5 0.1 copy.25
  10.6 0.2 reshape.130
  10.7 0.1 broadcast_in_dim.11
  10.8 0.2 reshape.129
  11.0 14.8 %convolution_bitcast_fusion.2 = f32[16,5,5,128,128]{3,4,1,2,0:T(8,128)} fusion(f32[16,128]{1,0:T(8,128)S(1)} %bitcast_convert_fusion.2, bf16[4,16,5,128,128]{4,3,2,1,0:T(8,128)(2,1)} %get-tuple-element.92, s32[]{:T(128)S(6)} %copy.30), kind=kOutput, calls=%fused_computation.1.clone.1 | convolution fusion | flops 1681653760 | bytes 31466496 | tf_op jit(solution)/shard_map/while/body/eval_jaxpr/kpiv,kqjv->kpqij/dot_general | solution.py:22
  25.8 27.4 %copy.26 = f32[16,5,5,128,128]{4,3,2,1,0:T(8,128)} copy(f32[16,5,5,128,128]{3,4,1,2,0:T(8,128)} %convolution_bitcast_fusion.2) | data formatting | bytes 52428800 | tf_op jit(solution)/shard_map/while/body/eval_jaxpr/kpiv,kqjv->kpqij/transpose | solution.py:22
  53.1 85.4 %scatter_fusion = f32[8,128,8,128]{3,1,2,0:T(8,128)} fusion(f32[8,128,8,128]{3,1,2,0:T(8,128)} %get-tuple-element.84, s32[400]{0:T(512)S(1)} %bitcast.53, f32[400,128,128]{2,1,0:T(8,128)} %bitcast.52), kind=kCustom, calls=%fused_computation.clone.1 | custom fusion | flops 6553600 | bytes 78646400 | tf_op jit(solution)/shard_map/while/body/eval_jaxpr/scatter-add | solution.py:31
  138.5 0.1 copy.25
  138.6 0.2 reshape.130
  138.8 0.1 broadcast_in_dim.11
  138.9 0.2 reshape.129
  139.1 14.8 %convolution_bitcast_fusion.2 = f32[16,5,5,128,128]{3,4,1,2,0:T(8,128)} fusion(f32[16,128]{1,0:T(8,128)S(1)} %bitcast_convert_fusion.2, bf16[4,16,5,128,128]{4,3,2,1,0:T(8,128)(2,1)} %get-tuple-element.92, s32[]{:T(128)S(6)} %copy.30), kind=kOutput, calls=%fused_computation.1.clone.1 | convolution fusion | flops 1681653760 | bytes 31466496 | tf_op jit(solution)/shard_map/while/body/eval_jaxpr/kpiv,kqjv->kpqij/dot_general | solution.py:22
  153.8 27.4 %copy.26 = f32[16,5,5,128,128]{4,3,2,1,0:T(8,128)} copy(f32[16,5,5,128,128]{3,4,1,2,0:T(8,128)} %convolution_bitcast_fusion.2) | data formatting | bytes 52428800 | tf_op jit(solution)/shard_map/while/body/eval_jaxpr/kpiv,kqjv->kpqij/transpose | solution.py:22
  181.2 85.5 %scatter_fusion = f32[8,128,8,128]{3,1,2,0:T(8,128)} fusion(f32[8,128,8,128]{3,1,2,0:T(8,128)} %get-tuple-element.84, s32[400]{0:T(512)S(1)} %bitcast.53, f32[400,128,128]{2,1,0:T(8,128)} %bitcast.52), kind=kCustom, calls=%fused_computation.clone.1 | custom fusion | flops 6553600 | bytes 78646400 | tf_op jit(solution)/shard_map/while/body/eval_jaxpr/scatter-add | solution.py:31
  266.8 0.1 copy.25
  266.8 0.2 reshape.130
  267.0 0.1 broadcast_in_dim.11
  267.1 0.2 reshape.129
  267.3 14.8 %convolution_bitcast_fusion.2 = f32[16,5,5,128,128]{3,4,1,2,0:T(8,128)} fusion(f32[16,128]{1,0:T(8,128)S(1)} %bitcast_convert_fusion.2, bf16[4,16,5,128,128]{4,3,2,1,0:T(8,128)(2,1)} %get-tuple-element.92, s32[]{:T(128)S(6)} %copy.30), kind=kOutput, calls=%fused_computation.1.clone.1 | convolution fusion | flops 1681653760 | bytes 31466496 | tf_op jit(solution)/shard_map/while/body/eval_jaxpr/kpiv,kqjv->kpqij/dot_general | solution.py:22
  282.1 27.4 %copy.26 = f32[16,5,5,128,128]{4,3,2,1,0:T(8,128)} copy(f32[16,5,5,128,128]{3,4,1,2,0:T(8,128)} %convolution_bitcast_fusion.2) | data formatting | bytes 52428800 | tf_op jit(solution)/shard_map/while/body/eval_jaxpr/kpiv,kqjv->kpqij/transpose | solution.py:22
  309.4 85.5 %scatter_fusion = f32[8,128,8,128]{3,1,2,0:T(8,128)} fusion(f32[8,128,8,128]{3,1,2,0:T(8,128)} %get-tuple-element.84, s32[400]{0:T(512)S(1)} %bitcast.53, f32[400,128,128]{2,1,0:T(8,128)} %bitcast.52), kind=kCustom, calls=%fused_computation.clone.1 | custom fusion | flops 6553600 | bytes 78646400 | tf_op jit(solution)/shard_map/while/body/eval_jaxpr/scatter-add | solution.py:31
  395.0 0.1 copy.25
  395.1 0.2 reshape.130
  395.2 0.1 broadcast_in_dim.11
  395.3 0.2 reshape.129
  395.5 14.8 %convolution_bitcast_fusion.2 = f32[16,5,5,128,128]{3,4,1,2,0:T(8,128)} fusion(f32[16,128]{1,0:T(8,128)S(1)} %bitcast_convert_fusion.2, bf16[4,16,5,128,128]{4,3,2,1,0:T(8,128)(2,1)} %get-tuple-element.92, s32[]{:T(128)S(6)} %copy.30), kind=kOutput, calls=%fused_computation.1.clone.1 | convolution fusion | flops 1681653760 | bytes 31466496 | tf_op jit(solution)/shard_map/while/body/eval_jaxpr/kpiv,kqjv->kpqij/dot_general | solution.py:22
  410.3 27.4 %copy.26 = f32[16,5,5,128,128]{4,3,2,1,0:T(8,128)} copy(f32[16,5,5,128,128]{3,4,1,2,0:T(8,128)} %convolution_bitcast_fusion.2) | data formatting | bytes 52428800 | tf_op jit(solution)/shard_map/while/body/eval_jaxpr/kpiv,kqjv->kpqij/transpose | solution.py:22
  437.6 85.4 %scatter_fusion = f32[8,128,8,128]{3,1,2,0:T(8,128)} fusion(f32[8,128,8,128]{3,1,2,0:T(8,128)} %get-tuple-element.84, s32[400]{0:T(512)S(1)} %bitcast.53, f32[400,128,128]{2,1,0:T(8,128)} %bitcast.52), kind=kCustom, calls=%fused_computation.clone.1 | custom fusion | flops 6553600 | bytes 78646400 | tf_op jit(solution)/shard_map/while/body/eval_jaxpr/scatter-add | solution.py:31
  523.0 4.6 copy.15
  527.6 2.9 copy.22
  530.5 0.0 copy-start
  530.5 0.0 reduce-scatter.2.cloned.1.call-update
  530.6 1.4 collective-permute-start
  532.0 0.1 copy-done
  532.1 4.3 collective-permute-start.1
  536.4 1.6 fusion.8
  538.0 0.0 copy-start.1
  538.0 0.0 collective-permute-done
  538.0 1.6 copy-done.1
  539.6 0.0 slice-start
  539.6 2.9 add_convert_fusion
  542.5 0.0 collective-permute-done.1
  542.5 0.0 slice-done
  542.5 2.9 fusion.17
  545.4 632.3 %reduce-scatter.2.cloned.1.call-done = f32[8,1024]{1,0:T(8,128)} async-done(((f32[1024,1024]{1,0:T(8,128)}), f32[8,1024]{1,0:T(8,128)}) %reduce-scatter.2.cloned.1.call-update) | async-done | bytes 32784 | tf_op jit(solution)/shard_map/reduce_scatter | solution.py:52
  (20 shorter events, 0.1 us)
Async XLA Ops:
  7.2 3.3 copy-start.2
  7.2 1170.5 %reduce-scatter.2.cloned.1.call-start = ((), (), s32[]{:S(2)}) async-start(), calls=%async_computation.1 | async-start | bytes 4227072 | tf_op jit(solution)/shard_map/reduce_scatter | solution.py:52
  530.5 1.6 copy-start
  530.6 7.4 collective-permute-start
  532.1 10.4 collective-permute-start.1
  538.0 1.6 copy-start.1
  539.6 2.9 slice-start
Sparse Core Ops, SparseCore 0:
  530.7 646.9 reduce-scatter.1
where the time goes:
time: 1190 us; the launch traced here: 1180 us
  waiting for transfers between devices  632 us (53%)
  other arithmetic  342 us (29%)
  local copies, waits for them, and re-layouts  124 us (10%)
  matrix products  66.4 us (6%)
  between operations  14.1 us (1%)
    reduce_scatter x1, waiting for transfers between devices, body(): lax.psum_scatter(flat_sum, ('var', 'own', 'sub'), scatter_dimension=0, ti...  632 us
    scatter-add x4, other arithmetic, accumulate(): partial_value.at[left_rows, :, right_rows, :]  342 us
    transpose x4, local copies, waits for them, and re-layouts, accumulate(): jnp.einsum('kpiv,kqjv->kpqij', scaled, blocks, preferred_element_type=jnp...  109 us
    dot_general x4, matrix products, accumulate(): jnp.einsum('kpiv,kqjv->kpqij', scaled, blocks, preferred_element_type=jnp...  59.1 us
  transfers between devices with their start and end apart: 3, of which 1 were waited for; matrix products, arithmetic and copies ran while one was open for 1% of the time, Pallas kernels for 0%

commit v1 on v0

v1 whole, which is shorter than its diff:
```python
import functools

import jax
import jax.numpy as jnp
from jax import lax
from jax.experimental import pallas as pl
from jax.experimental.pallas import tpu as pltpu
from jax.sharding import PartitionSpec as P

MESH = pl.DeviceIdType.MESH
CAP = 8
TILE = 256
ORDER = (2, 1, 3, 0)
CHUNKS = 4
BATCHES = (
    ((0, 0), (0, 1), (0, 2), (0, 3), (1, 0), (2, 0), (3, 0)),
    ((1, 1), (1, 2), (1, 3), (2, 1), (3, 1)),
    ((2, 2), (2, 3), (3, 2)),
    ((3, 3),),
)
NT = (((1,), (1,)), ((), ()))


def kernel(sizes, cap_ref, rows_ref, self_ref, prev_ref, scal_ref, diag_ref, lower_ref, norm_ref, *scratch):
    local, per_block, edge = sizes
    group = local // CHUNKS
    scratch = list(scratch)
    raws = [scratch.pop(0) for _ in range(CHUNKS)]
    panels = [scratch.pop(0) for _ in range(CHUNKS)]
    core_send = [scratch.pop(0) for _ in range(4)]
    core_recv = [scratch.pop(0) for _ in range(4)]
    plane_send = [scratch.pop(0) for _ in range(4)]
    plane_recv = [scratch.pop(0) for _ in range(4)]
    (acc, root, dsc, cself, cprev, cdiag, clower, bnd_block, bnd_scale, ysum, yrecv, out_buf) = scratch[:12]
    (load_sem, cover_sem, out_sem, norm_sem, bnd_send, bnd_recv, core_ssem, core_rsem,
     plane_ssem, plane_rsem, y_ssem, y_rsem) = scratch[12:]

    var, own, sub = lax.axis_index("var"), lax.axis_index("own"), lax.axis_index("sub")
    y, z, x = var // 4, var % 4, own
    here = (var * 4 + own) * 2 + sub

    def device(index):
        return (index // 8, (index // 2) % 4, index % 2)

    after, before = device((here + 1) % 128), device((here + 127) % 128)
    other = (var, own, 1 - sub)

    def plane_peer(d):
        return (y * 4 + (z + d // 4) % 4, (x + d % 4) % 4, sub)

    def y_peer(t):
        return (((y + ORDER[t]) % 4) * 4 + z, x, sub)

    barrier = pltpu.get_barrier_semaphore()

    loads = []
    for c in range(CHUNKS):
        copy = pltpu.make_async_copy(
            cap_ref.at[pl.ds(c * group * per_block, group * per_block)],
            raws[c].at[pl.ds(0, group * per_block)],
            load_sem.at[c],
        )
        loads.append(copy)
    cover_loads = [
        pltpu.make_async_copy(self_ref, cself.at[pl.ds(1, local)], cover_sem.at[0]),
        pltpu.make_async_copy(prev_ref, cprev, cover_sem.at[1]),
    ]
    loads[0].start()
    loads[1].start()

    for peer in (other, after, before):
        pl.semaphore_signal(barrier, inc=1, device_id=peer, device_id_type=MESH)
    for t in range(3):
        pl.semaphore_signal(barrier, inc=1, device_id=y_peer(t), device_id_type=MESH)

    @pl.loop(1, 16)
    def _(d):
        pl.semaphore_signal(barrier, inc=1, device_id=plane_peer(d), device_id_type=MESH)

    for c in range(CHUNKS):
        raws[c][group * per_block] = jnp.zeros((edge, edge), jnp.bfloat16)
    scale = scal_ref[...].astype(jnp.float32)
    dsc[pl.ds(8, local), :] = scale
    root[...] = jnp.sqrt(scale)

    def build(c):
        @pl.loop(0, group)
        def _(kk):
            k = c * group + kk
            named = [rows_ref[k, p] for p in range(per_block)]
            d = root[pl.ds(k, 1), :]
            column = pl.ds(pl.multiple_of(kk * edge, edge), edge)
            for t in range(4):
                for h in range(2):
                    row = ((y + ORDER[t]) % 4) * 2 + h
                    at = jnp.int32(group * per_block)
                    for p in range(per_block):
                        at = jnp.where(named[p] == row, kk * per_block + p, at)
                    block = raws[c][at]
                    panels[c][pl.ds((t * 2 + h) * edge, edge), column] = (
                        block.astype(jnp.float32) * d
                    ).astype(jnp.bfloat16)

    def product(c, t, j):
        part = lax.dot_general(
            panels[c][pl.ds(t * TILE, TILE), :],
            panels[c][pl.ds(j * TILE, TILE), :],
            NT,
            preferred_element_type=jnp.float32,
        )
        unit = (pl.ds(t * TILE, TILE), pl.ds(j * TILE, TILE))
        if c == 0:
            acc[unit] = part
        else:
            acc[unit] += part

    def unit_of(t, j):
        for c in range(CHUNKS):
            product(c, t, j)

    core_copies = [
        pltpu.make_async_remote_copy(
            src_ref=core_send[b].at[1 - sub],
            dst_ref=core_recv[b],
            send_sem=core_ssem.at[b],
            recv_sem=core_rsem.at[b],
            device_id=other,
            device_id_type=MESH,
        )
        for b in range(4)
    ]

    def pack(b):
        for u, (t, j) in enumerate(BATCHES[b]):
            if t <= j:
                value = acc[pl.ds(t * TILE, TILE), pl.ds(j * TILE, TILE)]
            else:
                value = acc[pl.ds(j * TILE, TILE), pl.ds(t * TILE, TILE)].T
            value = value.reshape(16, 2, 8, TILE).astype(jnp.bfloat16)
            for c in range(2):
                core_send[b][c, :, pl.ds(u * 8, 8), :] = value[:, c]
        core_copies[b].start()

    def plane_copy(b, d):
        to = ((z + d // 4) % 4) * 4 + (x + d % 4) % 4
        return pltpu.make_async_remote_copy(
            src_ref=plane_send[b].at[to],
            dst_ref=plane_recv[b].at[d],
            send_sem=plane_ssem.at[b, d],
            recv_sem=plane_rsem.at[b, d],
            device_id=plane_peer(d),
            device_id_type=MESH,
        )

    def add_core(b):
        core_copies[b].wait_recv()
        plane_send[b][...] = (
            core_send[b][sub].astype(jnp.float32) + core_recv[b][...].astype(jnp.float32)
        ).astype(jnp.bfloat16)

        @pl.loop(1, 16)
        def _(d):
            plane_copy(b, d).start()

    y_copies = [
        pltpu.make_async_remote_copy(
            src_ref=ysum.at[t],
            dst_ref=yrecv.at[t],
            send_sem=y_ssem.at[t],
            recv_sem=y_rsem.at[t],
            device_id=y_peer(t),
            device_id_type=MESH,
        )
        for t in range(3)
    ]

    def add_plane(b):
        @pl.loop(1, 16)
        def _(d):
            plane_copy(b, d).wait_recv()

        total = plane_send[b][z * 4 + x].astype(jnp.float32)
        for d in range(1, 16):
            total = total + plane_recv[b][d].astype(jnp.float32)
        for u, (t, j) in enumerate(BATCHES[b]):
            column = pl.multiple_of(((y + ORDER[j]) % 4) * TILE, TILE)
            ysum[t, :, pl.ds(column, TILE)] = total[u * 8 : (u + 1) * 8]
        if b < 3:
            y_copies[b].start()

    def cover(c):
        @pl.loop(c * group, (c + 1) * group)
        def _(k):
            d = dsc[pl.ds(k + 8, 1), :].astype(jnp.bfloat16)
            d_prev = dsc[pl.ds(k + 7, 1), :].astype(jnp.bfloat16)
            block, link = cself[k + 1], cprev[k]
            scaled, scaled_link = block * d, link * d_prev
            total = lax.dot_general(
                jnp.concatenate([scaled, scaled_link], axis=1),
                jnp.concatenate([block, link], axis=1),
                NT,
                preferred_element_type=jnp.float32,
            )
            cdiag[k] = total.astype(jnp.bfloat16)
            clower[k] = lax.dot_general(
                scaled_link, cself[k], NT, preferred_element_type=jnp.float32
            ).astype(jnp.bfloat16)

        part = pl.ds(c * group, group)
        copies = [
            pltpu.make_async_copy(cdiag.at[part], diag_ref.at[part], out_sem.at[0, c]),
            pltpu.make_async_copy(clower.at[part], lower_ref.at[part], out_sem.at[1, c]),
        ]
        for copy in copies:
            copy.start()
        return copies

    for c in range(CHUNKS):
        loads[c].wait()
        if c + 2 < CHUNKS:
            loads[c + 2].start()
        elif c + 2 == CHUNKS:
            cover_loads[0].start()
            cover_loads[1].start()
        build(c)
        for j in range(4):
            product(c, 0, j)

    pl.semaphore_wait(barrier, 21)
    boundary = [
        pltpu.make_async_remote_copy(
            src_ref=self_ref.at[local - 1],
            dst_ref=bnd_block,
            send_sem=bnd_send.at[0],
            recv_sem=bnd_recv.at[0],
            device_id=after,
            device_id_type=MESH,
        ),
        pltpu.make_async_remote_copy(
            src_ref=scal_ref.at[pl.ds(local - 16, 16)],
            dst_ref=bnd_scale,
            send_sem=bnd_send.at[1],
            recv_sem=bnd_recv.at[1],
            device_id=after,
            device_id_type=MESH,
        ),
    ]
    for copy in boundary:
        copy.start()
    pack(0)
    unit_of(1, 1)
    add_core(0)
    unit_of(1, 2)
    unit_of(1, 3)
    pack(1)
    unit_of(2, 2)
    add_core(1)
    unit_of(2, 3)
    pack(2)
    unit_of(3, 3)
    pack(3)
    add_core(2)

    for copy in cover_loads:
        copy.wait()
    for copy in boundary:
        copy.wait_recv()
    first = here == 0
    cself[0] = jnp.where(first, jnp.zeros_like(bnd_block), bnd_block[...])
    dsc[pl.ds(7, 1), :] = jnp.where(first, 0.0, bnd_scale[...].astype(jnp.float32)[15:16, :])

    outs = []
    outs += cover(0)
    add_core(3)
    add_plane(0)
    outs += cover(1)
    add_plane(1)
    outs += cover(2)
    add_plane(2)
    outs += cover(3)
    add_plane(3)
    total = ysum[3]
    for t in range(3):
        y_copies[t].wait_recv()
        total = total + yrecv[t]
    out_buf[...] = total
    last = pltpu.make_async_copy(out_buf, norm_ref, norm_sem)
    last.start()
    for copy in boundary + core_copies + y_copies:
        copy.wait_send()
    for b in range(4):
        @pl.loop(1, 16)
        def _(d):
            plane_copy(b, d).wait_send()
    for copy in outs:
        copy.wait()
    last.wait()


def body(capacity_blocks, capacity_rows, cover_self, cover_prev, scaling):
    local, per_block, edge, _ = capacity_blocks.shape
    group = local // CHUNKS
    full = CAP * edge
    bf16, f32 = jnp.bfloat16, jnp.float32
    counts = [len(batch) for batch in BATCHES]
    dma = pltpu.SemaphoreType.DMA
    scratch = [pltpu.VMEM((group * per_block + 1, edge, edge), bf16) for _ in range(CHUNKS)]
    scratch += [pltpu.VMEM((full, group * edge), bf16) for _ in range(CHUNKS)]
    scratch += [pltpu.VMEM((2, 16, n * 8, TILE), bf16) for n in counts]
    scratch += [pltpu.VMEM((16, n * 8, TILE), bf16) for n in counts]
    scratch += [pltpu.VMEM((16, n * 8, TILE), bf16) for n in counts]
    scratch += [pltpu.VMEM((16, n * 8, TILE), bf16) for n in counts]
    scratch += [
        pltpu.VMEM((full, full), f32),
        pltpu.VMEM((local, edge), f32),
        pltpu.VMEM((local + 8, edge), f32),
        pltpu.VMEM((local + 1, edge, edge), bf16),
        pltpu.VMEM((local, edge, edge), bf16),
        pltpu.VMEM((local, edge, edge), bf16),
        pltpu.VMEM((local, edge, edge), bf16),
        pltpu.VMEM((edge, edge), bf16),
        pltpu.VMEM((16, edge), bf16),
        pltpu.VMEM((4, 8, full), f32),
        pltpu.VMEM((3, 8, full), f32),
        pltpu.VMEM((8, full), f32),
    ]
    scratch += [
        dma((CHUNKS,)), dma((2,)), dma((2, CHUNKS)), dma(()), dma((2,)), dma((2,)),
        dma((4,)), dma((4,)), dma((4, 16)), dma((4, 16)), dma((3,)), dma((3,)),
    ]
    anywhere = pl.BlockSpec(memory_space=pl.ANY)
    return pl.pallas_call(
        functools.partial(kernel, (local, per_block, edge)),
        out_shape=(
            jax.ShapeDtypeStruct((local, edge, edge), bf16),
            jax.ShapeDtypeStruct((local, edge, edge), bf16),
            jax.ShapeDtypeStruct((8, full), f32),
        ),
        in_specs=[
            anywhere,
            pl.BlockSpec(memory_space=pltpu.SMEM),
            anywhere,
            anywhere,
            pl.BlockSpec(memory_space=pltpu.VMEM),
        ],
        out_specs=(anywhere, anywhere, anywhere),
        scratch_shapes=scratch,
        compiler_params=pltpu.CompilerParams(
            collective_id=0, has_side_effects=True, vmem_limit_bytes=60 << 20
        ),
    )(capacity_blocks.reshape(local * per_block, edge, edge), capacity_rows, cover_self, cover_prev, scaling)


def solution(mesh):
    axes = ("var", "own", "sub")
    placed = (P(axes, None, None, None), P(axes, None), P(axes, None, None), P(axes, None, None), P(axes, None))
    return jax.shard_map(
        body,
        mesh=mesh,
        in_specs=placed,
        out_specs=(P(axes, None, None), P(axes, None, None), P(axes, None)),
        check_vma=False,
    )
```

time: 1190 us -> 49.6 us (0.04)
  waiting for transfers between devices: 632 us -> 0 us
  other arithmetic: 342 us -> 0 us
  local copies, waits for them, and re-layouts: 124 us -> 6.64 us
  matrix products: 66.4 us -> 0 us
  Pallas kernels: 0 us -> 41.8 us
  between operations: 14.1 us -> 0.65 us
    reduce_scatter x1 -> x0, waiting for transfers between devices: 632 us -> none  [body(): lax.psum_scatter(flat_sum, ('var', 'own', 'sub'), scatter_dimension=0, ti...]
    scatter-add x4 -> x0, other arithmetic: 342 us -> none  [accumulate(): partial_value.at[left_rows, :, right_rows, :]]
    transpose x4 -> x0, local copies, waits for them, and re-layouts: 109 us -> none  [accumulate(): jnp.einsum('kpiv,kqjv->kpqij', scaled, blocks, preferred_element_type=jnp...]
    dot_general x7 -> x0, matrix products: 66.4 us -> none  [the longest x4 59.1 us: accumulate(): jnp.einsum('kpiv,kqjv->kpqij', scaled, blocks, preferred_element_type=jnp...]
    pallas_call x0 -> x1, Pallas kernels: none -> 41.8 us  [body(): pl.pallas_call(functools.partial(kernel, (local, per_block, edge)), out_s...]
  transfers between devices with their start and end apart: 3 -> 0, of which waited for: 1 -> 0; matrix products, arithmetic and copies ran while one was open for 1% -> 0% of each run, Pallas kernels for 0% -> 0%
where the time goes in v1:
time: 49.6 us; the launch traced here: 49.1 us
  Pallas kernels  41.8 us (84%)
  local copies, waits for them, and re-layouts  6.64 us (13%)
  between operations  0.65 us (1%)
    pallas_call x1, Pallas kernels, body(): pl.pallas_call(functools.partial(kernel, (local, per_block, edge)), out_s...  41.8 us
    unnamed x8, local copies, waits for them, and re-layouts  6.64 us

profile of v1, /device:TPU:0, one launch (start us, length us, event | category | flops | bytes accessed | tf_op | source)
XLA Modules:
  0.0 49.1 jit_solution(8232022232494490013)
XLA Ops:
  0.6 1.4 %copy.8.rows_ref = s32[64,5]{1,0:T(8,128)} copy(s32[64,5]{0,1:T(8,128)} %param.6) | data formatting | bytes 2560 | tf_op args[1]
  2.0 41.8 %shard_map.76 = (bf16[64,128,128]{2,1,0:T(8,128)(2,1)}, bf16[64,128,128]{2,1,0:T(8,128)(2,1)}, f32[8,1024]{1,0:T(8,128)}) custom-call(bf16[320,128,128]{2,1,0:T(8,128)(2,1)} %bitcast.1, s32[64,5]{1,0:T(8,128)} %copy.8.rows_ref, bf16[64,128,128]{2,1,0:T(8,128)(2,1)} %self_ref.1, bf16[64,128,128]{2,1,0:T(8,128)(2,1)} %prev_ref.1, bf16[64,128]{1,0:T(8,128)(2,1)} %scal_ref.1), custom_call_target="tpu_custom_call" | custom-call | tf_op jit(solution)/shard_map/pallas_call | solution.py:332
  43.9 0.0 copy-start
  43.9 3.3 %copy.12 = bf16[64,128,128]{2,1,0:T(8,128)(2,1)} copy(bf16[64,128,128]{2,1,0:T(8,128)(2,1)} %get-tuple-element.6) | data formatting | bytes 4194304
  47.2 0.0 copy-done
  47.2 0.0 copy-start.1
  47.2 1.3 %copy.13 = bf16[64,128,128]{2,1,0:T(8,128)(2,1)} copy(bf16[64,128,128]{2,1,0:T(8,128)(2,1)S(1)} %copy-done) | data formatting | bytes 4194304
  48.5 0.0 copy-done.1
  48.5 0.6 %copy.14 = f32[8,1024]{1,0:T(8,128)} copy(f32[8,1024]{1,0:T(8,128)S(1)} %copy-done.1) | data formatting | bytes 65536
Async XLA Ops:
  43.9 3.3 %copy-start = (bf16[64,128,128]{2,1,0:T(8,128)(2,1)S(1)}, bf16[64,128,128]{2,1,0:T(8,128)(2,1)}, u32[]{:S(2)}) copy-start(bf16[64,128,128]{2,1,0:T(8,128)(2,1)} %get-tuple-element.7) | copy-start | bytes 6291460
  47.2 1.3 %copy-start.1 = (f32[8,1024]{1,0:T(8,128)S(1)}, f32[8,1024]{1,0:T(8,128)}, u32[]{:S(2)}) copy-start(f32[8,1024]{1,0:T(8,128)} %get-tuple-element.8) | copy-start | bytes 98308

commit v2 on v1

--- a/solution.py
+++ b/solution.py
@@ -11,7 +11,8 @@
 CAP = 8
 TILE = 256
 ORDER = (2, 1, 3, 0)
-CHUNKS = 4
+CHUNKS = (8, 16, 20, 20)
+STARTS = (0, 8, 24, 44)
 BATCHES = (
     ((0, 0), (0, 1), (0, 2), (0, 3), (1, 0), (2, 0), (3, 0)),
     ((1, 1), (1, 2), (1, 3), (2, 1), (3, 1)),
@@ -23,17 +24,17 @@
 
 def kernel(sizes, cap_ref, rows_ref, self_ref, prev_ref, scal_ref, diag_ref, lower_ref, norm_ref, *scratch):
     local, per_block, edge = sizes
-    group = local // CHUNKS
+    group = local // 4
     scratch = list(scratch)
-    raws = [scratch.pop(0) for _ in range(CHUNKS)]
-    panels = [scratch.pop(0) for _ in range(CHUNKS)]
+    raws = [scratch.pop(0) for _ in CHUNKS]
+    scaled_raws = [scratch.pop(0) for _ in CHUNKS]
     core_send = [scratch.pop(0) for _ in range(4)]
     core_recv = [scratch.pop(0) for _ in range(4)]
     plane_send = [scratch.pop(0) for _ in range(4)]
     plane_recv = [scratch.pop(0) for _ in range(4)]
-    (acc, root, dsc, cself, cprev, cdiag, clower, bnd_block, bnd_scale, ysum, yrecv, out_buf) = scratch[:12]
-    (load_sem, cover_sem, out_sem, norm_sem, bnd_send, bnd_recv, core_ssem, core_rsem,
-     plane_ssem, plane_rsem, y_ssem, y_rsem) = scratch[12:]
+    (acc, dsc, cself, cprev, bnd_block, bnd_scale, ysum, yrecv) = scratch[:8]
+    (load_sem, cover_sem, bnd_send, bnd_recv, core_ssem, core_rsem,
+     plane_ssem, plane_rsem, y_ssem, y_rsem) = scratch[8:]
 
     var, own, sub = lax.axis_index("var"), lax.axis_index("own"), lax.axis_index("sub")
     y, z, x = var // 4, var % 4, own
@@ -54,10 +55,10 @@
     barrier = pltpu.get_barrier_semaphore()
 
     loads = []
-    for c in range(CHUNKS):
+    for c, size in enumerate(CHUNKS):
         copy = pltpu.make_async_copy(
-            cap_ref.at[pl.ds(c * group * per_block, group * per_block)],
-            raws[c].at[pl.ds(0, group * per_block)],
+            cap_ref.at[pl.ds(STARTS[c] * per_block, size * per_block)],
+            raws[c].at[pl.ds(0, size * per_block)],
             load_sem.at[c],
         )
         loads.append(copy)
@@ -65,8 +66,8 @@
         pltpu.make_async_copy(self_ref, cself.at[pl.ds(1, local)], cover_sem.at[0]),
         pltpu.make_async_copy(prev_ref, cprev, cover_sem.at[1]),
     ]
-    loads[0].start()
-    loads[1].start()
+    for copy in loads:
+        copy.start()
 
     for peer in (other, after, before):
         pl.semaphore_signal(barrier, inc=1, device_id=peer, device_id_type=MESH)
@@ -77,36 +78,41 @@
     def _(d):
         pl.semaphore_signal(barrier, inc=1, device_id=plane_peer(d), device_id_type=MESH)
 
-    for c in range(CHUNKS):
-        raws[c][group * per_block] = jnp.zeros((edge, edge), jnp.bfloat16)
-    scale = scal_ref[...].astype(jnp.float32)
-    dsc[pl.ds(8, local), :] = scale
-    root[...] = jnp.sqrt(scale)
-
-    def build(c):
-        @pl.loop(0, group)
-        def _(kk):
-            k = c * group + kk
-            named = [rows_ref[k, p] for p in range(per_block)]
-            d = root[pl.ds(k, 1), :]
-            column = pl.ds(pl.multiple_of(kk * edge, edge), edge)
+    blank = jnp.zeros((edge, edge), jnp.bfloat16)
+    for c, size in enumerate(CHUNKS):
+        raws[c][size * per_block] = blank
+        scaled_raws[c][size * per_block] = blank
+    dsc[pl.ds(8, local), :] = scal_ref[...].astype(jnp.float32)
+
+    places = {}
+
+    def place(c):
+        for kk in range(CHUNKS[c]):
+            named = [rows_ref[p, STARTS[c] + kk] for p in range(per_block)]
             for t in range(4):
                 for h in range(2):
                     row = ((y + ORDER[t]) % 4) * 2 + h
-                    at = jnp.int32(group * per_block)
+                    at = jnp.int32(CHUNKS[c] * per_block)
                     for p in range(per_block):
                         at = jnp.where(named[p] == row, kk * per_block + p, at)
-                    block = raws[c][at]
-                    panels[c][pl.ds((t * 2 + h) * edge, edge), column] = (
-                        block.astype(jnp.float32) * d
-                    ).astype(jnp.bfloat16)
+                    places[c, kk, t, h] = at
+
+    def apply_scale(c):
+        for kk in range(CHUNKS[c]):
+            d = dsc[pl.ds(8 + STARTS[c] + kk, 1), :].astype(jnp.bfloat16)
+            for p in range(per_block):
+                scaled_raws[c][kk * per_block + p] = raws[c][kk * per_block + p] * d
+
+    def operand(source, c, t):
+        halves = [
+            jnp.concatenate([source[c][places[c, kk, t, h]] for kk in range(CHUNKS[c])], axis=1)
+            for h in range(2)
+        ]
+        return jnp.concatenate(halves, axis=0)
 
     def product(c, t, j):
         part = lax.dot_general(
-            panels[c][pl.ds(t * TILE, TILE), :],
-            panels[c][pl.ds(j * TILE, TILE), :],
-            NT,
-            preferred_element_type=jnp.float32,
+            operand(scaled_raws, c, t), operand(raws, c, j), NT, preferred_element_type=jnp.float32
         )
         unit = (pl.ds(t * TILE, TILE), pl.ds(j * TILE, TILE))
         if c == 0:
@@ -115,7 +121,7 @@
             acc[unit] += part
 
     def unit_of(t, j):
-        for c in range(CHUNKS):
+        for c in range(len(CHUNKS)):
             product(c, t, j)
 
     core_copies = [
@@ -189,7 +195,7 @@
             y_copies[b].start()
 
     def cover(c):
-        @pl.loop(c * group, (c + 1) * group)
+        @pl.loop(c * group, (c + 1) * group, unroll=group)
         def _(k):
             d = dsc[pl.ds(k + 8, 1), :].astype(jnp.bfloat16)
             d_prev = dsc[pl.ds(k + 7, 1), :].astype(jnp.bfloat16)
@@ -201,28 +207,17 @@
                 NT,
                 preferred_element_type=jnp.float32,
             )
-            cdiag[k] = total.astype(jnp.bfloat16)
-            clower[k] = lax.dot_general(
+            diag_ref[k] = total.astype(jnp.bfloat16)
+            lower_ref[k] = lax.dot_general(
                 scaled_link, cself[k], NT, preferred_element_type=jnp.float32
             ).astype(jnp.bfloat16)
 
-        part = pl.ds(c * group, group)
-        copies = [
-            pltpu.make_async_copy(cdiag.at[part], diag_ref.at[part], out_sem.at[0, c]),
-            pltpu.make_async_copy(clower.at[part], lower_ref.at[part], out_sem.at[1, c]),
-        ]
-        for copy in copies:
-            copy.start()
-        return copies
-
-    for c in range(CHUNKS):
+    for copy in cover_loads:
+        copy.start()
+    for c in range(len(CHUNKS)):
+        place(c)
         loads[c].wait()
-        if c + 2 < CHUNKS:
-            loads[c + 2].start()
-        elif c + 2 == CHUNKS:
-            cover_loads[0].start()
-            cover_loads[1].start()
-        build(c)
+        apply_scale(c)
         for j in range(4):
             product(c, 0, j)
 
@@ -269,72 +264,60 @@
     cself[0] = jnp.where(first, jnp.zeros_like(bnd_block), bnd_block[...])
     dsc[pl.ds(7, 1), :] = jnp.where(first, 0.0, bnd_scale[...].astype(jnp.float32)[15:16, :])
 
-    outs = []
-    outs += cover(0)
+    cover(0)
     add_core(3)
     add_plane(0)
-    outs += cover(1)
+    cover(1)
     add_plane(1)
-    outs += cover(2)
+    cover(2)
     add_plane(2)
-    outs += cover(3)
+    cover(3)
     add_plane(3)
     total = ysum[3]
     for t in range(3):
         y_copies[t].wait_recv()
         total = total + yrecv[t]
-    out_buf[...] = total
-    last = pltpu.make_async_copy(out_buf, norm_ref, norm_sem)
-    last.start()
+    norm_ref[...] = total
     for copy in boundary + core_copies + y_copies:
         copy.wait_send()
     for b in range(4):
         @pl.loop(1, 16)
         def _(d):
             plane_copy(b, d).wait_send()
-    for copy in outs:
-        copy.wait()
-    last.wait()
 
 
 def body(capacity_blocks, capacity_rows, cover_self, cover_prev, scaling):
     local, per_block, edge, _ = capacity_blocks.shape
-    group = local // CHUNKS
     full = CAP * edge
     bf16, f32 = jnp.bfloat16, jnp.float32
     counts = [len(batch) for batch in BATCHES]
     dma = pltpu.SemaphoreType.DMA
-    scratch = [pltpu.VMEM((group * per_block + 1, edge, edge), bf16) for _ in range(CHUNKS)]
-    scratch += [pltpu.VMEM((full, group * edge), bf16) for _ in range(CHUNKS)]
+    scratch = [pltpu.VMEM((n * per_block + 1, edge, edge), bf16) for n in CHUNKS * 2]
     scratch += [pltpu.VMEM((2, 16, n * 8, TILE), bf16) for n in counts]
     scratch += [pltpu.VMEM((16, n * 8, TILE), bf16) for n in counts]
     scratch += [pltpu.VMEM((16, n * 8, TILE), bf16) for n in counts]
     scratch += [pltpu.VMEM((16, n * 8, TILE), bf16) for n in counts]
     scratch += [
         pltpu.VMEM((full, full), f32),
-        pltpu.VMEM((local, edge), f32),
         pltpu.VMEM((local + 8, edge), f32),
         pltpu.VMEM((local + 1, edge, edge), bf16),
-        pltpu.VMEM((local, edge, edge), bf16),
-        pltpu.VMEM((local, edge, edge), bf16),
         pltpu.VMEM((local, edge, edge), bf16),
         pltpu.VMEM((edge, edge), bf16),
         pltpu.VMEM((16, edge), bf16),
         pltpu.VMEM((4, 8, full), f32),
         pltpu.VMEM((3, 8, full), f32),
-        pltpu.VMEM((8, full), f32),
     ]
     scratch += [
-        dma((CHUNKS,)), dma((2,)), dma((2, CHUNKS)), dma(()), dma((2,)), dma((2,)),
+        dma((len(CHUNKS),)), dma((2,)), dma((2,)), dma((2,)),
         dma((4,)), dma((4,)), dma((4, 16)), dma((4, 16)), dma((3,)), dma((3,)),
     ]
     anywhere = pl.BlockSpec(memory_space=pl.ANY)
     return pl.pallas_call(
         functools.partial(kernel, (local, per_block, edge)),
         out_shape=(
-            jax.ShapeDtypeStruct((local, edge, edge), bf16),
-            jax.ShapeDtypeStruct((local, edge, edge), bf16),
-            jax.ShapeDtypeStruct((8, full), f32),
+            pltpu.VMEM((local, edge, edge), bf16),
+            pltpu.VMEM((local, edge, edge), bf16),
+            pltpu.VMEM((8, full), f32),
         ),
         in_specs=[
             anywhere,
@@ -343,12 +326,12 @@
             anywhere,
             pl.BlockSpec(memory_space=pltpu.VMEM),
         ],
-        out_specs=(anywhere, anywhere, anywhere),
+        out_specs=(pl.BlockSpec(memory_space=pltpu.VMEM),) * 3,
         scratch_shapes=scratch,
         compiler_params=pltpu.CompilerParams(
-            collective_id=0, has_side_effects=True, vmem_limit_bytes=60 << 20
+            collective_id=0, has_side_effects=True, vmem_limit_bytes=50 << 20
         ),
-    )(capacity_blocks.reshape(local * per_block, edge, edge), capacity_rows, cover_self, cover_prev, scaling)
+    )(capacity_blocks.reshape(local * per_block, edge, edge), capacity_rows.T, cover_self, cover_prev, scaling)
 
 
 def solution(mesh):

time: 49.6 us -> 41.6 us (0.84)
  Pallas kernels: 41.8 us -> 37.5 us
  local copies, waits for them, and re-layouts: 6.64 us -> 3.25 us
    pallas_call x1, Pallas kernels: 41.8 us -> 37.5 us  [body(): pl.pallas_call(functools.partial(kernel, (local, per_block, edge)), out_s...]
    unnamed x8 -> x3, local copies, waits for them, and re-layouts: 6.64 us -> 3.25 us
where the time goes in v2:
time: 41.6 us; the launch traced here: 41.4 us
  Pallas kernels  37.5 us (90%)
  local copies, waits for them, and re-layouts  3.25 us (8%)
  between operations  0.64 us (2%)
    pallas_call x1, Pallas kernels, body(): pl.pallas_call(functools.partial(kernel, (local, per_block, edge)), out_s...  37.5 us
    unnamed x3, local copies, waits for them, and re-layouts  3.25 us

profile of v2, /device:TPU:0, one launch (start us, length us, event | category | flops | bytes accessed | tf_op | source)
XLA Modules:
  0.0 41.4 jit_solution(11651700495732003109)
XLA Ops:
  0.6 37.5 %shard_map.76 = (bf16[64,128,128]{2,1,0:T(8,128)(2,1)S(1)}, bf16[64,128,128]{2,1,0:T(8,128)(2,1)S(1)}, f32[8,1024]{1,0:T(8,128)S(1)}) custom-call(bf16[320,128,128]{2,1,0:T(8,128)(2,1)} %bitcast.2, s32[5,64]{1,0:T(8,128)} %bitcast.3, bf16[64,128,128]{2,1,0:T(8,128)(2,1)} %self_ref.1, bf16[64,128,128]{2,1,0:T(8,128)(2,1)} %prev_ref.1, bf16[64,128]{1,0:T(8,128)(2,1)} %scal_ref.1), custom_call_target="tpu_custom_call" | custom-call | tf_op jit(solution)/shard_map/pallas_call | solution.py:315
  38.1 1.3 %copy.11 = bf16[64,128,128]{2,1,0:T(8,128)(2,1)} copy(bf16[64,128,128]{2,1,0:T(8,128)(2,1)S(1)} %get-tuple-element.3) | data formatting | bytes 4194304
  39.4 0.6 %copy.13 = f32[8,1024]{1,0:T(8,128)} copy(f32[8,1024]{1,0:T(8,128)S(1)} %get-tuple-element.5) | data formatting | bytes 65536
  40.1 1.3 %copy.12 = bf16[64,128,128]{2,1,0:T(8,128)(2,1)} copy(bf16[64,128,128]{2,1,0:T(8,128)(2,1)S(1)} %get-tuple-element.4) | data formatting | bytes 4194304

commit v3 on v2

--- a/solution.py
+++ b/solution.py
@@ -30,11 +30,13 @@
     scaled_raws = [scratch.pop(0) for _ in CHUNKS]
     core_send = [scratch.pop(0) for _ in range(4)]
     core_recv = [scratch.pop(0) for _ in range(4)]
-    plane_send = [scratch.pop(0) for _ in range(4)]
-    plane_recv = [scratch.pop(0) for _ in range(4)]
+    first_send = [scratch.pop(0) for _ in range(4)]
+    first_recv = [scratch.pop(0) for _ in range(4)]
+    second_send = [scratch.pop(0) for _ in range(4)]
+    second_recv = [scratch.pop(0) for _ in range(4)]
     (acc, dsc, cself, cprev, bnd_block, bnd_scale, ysum, yrecv) = scratch[:8]
     (load_sem, cover_sem, bnd_send, bnd_recv, core_ssem, core_rsem,
-     plane_ssem, plane_rsem, y_ssem, y_rsem) = scratch[8:]
+     first_ssem, first_rsem, second_ssem, second_rsem, y_ssem, y_rsem) = scratch[8:]
 
     var, own, sub = lax.axis_index("var"), lax.axis_index("own"), lax.axis_index("sub")
     y, z, x = var // 4, var % 4, own
@@ -46,8 +48,13 @@
     after, before = device((here + 1) % 128), device((here + 127) % 128)
     other = (var, own, 1 - sub)
 
-    def plane_peer(d):
-        return (y * 4 + (z + d // 4) % 4, (x + d % 4) % 4, sub)
+    my_first, my_second = z * (1 - sub) + x * sub, x * (1 - sub) + z * sub
+
+    def first_peer(d):
+        return (y * 4 + (z + d * (1 - sub)) % 4, (x + d * sub) % 4, sub)
+
+    def second_peer(d):
+        return (y * 4 + (z + d * sub) % 4, (x + d * (1 - sub)) % 4, sub)
 
     def y_peer(t):
         return (((y + ORDER[t]) % 4) * 4 + z, x, sub)
@@ -74,9 +81,9 @@
     for t in range(3):
         pl.semaphore_signal(barrier, inc=1, device_id=y_peer(t), device_id_type=MESH)
 
-    @pl.loop(1, 16)
-    def _(d):
-        pl.semaphore_signal(barrier, inc=1, device_id=plane_peer(d), device_id_type=MESH)
+    for d in range(1, 4):
+        pl.semaphore_signal(barrier, inc=1, device_id=first_peer(d), device_id_type=MESH)
+        pl.semaphore_signal(barrier, inc=1, device_id=second_peer(d), device_id_type=MESH)
 
     blank = jnp.zeros((edge, edge), jnp.bfloat16)
     for c, size in enumerate(CHUNKS):
@@ -147,26 +154,55 @@
                 core_send[b][c, :, pl.ds(u * 8, 8), :] = value[:, c]
         core_copies[b].start()
 
-    def plane_copy(b, d):
-        to = ((z + d // 4) % 4) * 4 + (x + d % 4) % 4
-        return pltpu.make_async_remote_copy(
-            src_ref=plane_send[b].at[to],
-            dst_ref=plane_recv[b].at[d],
-            send_sem=plane_ssem.at[b, d],
-            recv_sem=plane_rsem.at[b, d],
-            device_id=plane_peer(d),
-            device_id_type=MESH,
-        )
+    first_copies = [
+        [
+            pltpu.make_async_remote_copy(
+                src_ref=first_send[b].at[(my_first + d) % 4],
+                dst_ref=first_recv[b].at[d],
+                send_sem=first_ssem.at[b, d],
+                recv_sem=first_rsem.at[b, d],
+                device_id=first_peer(d),
+                device_id_type=MESH,
+            )
+            for d in range(1, 4)
+        ]
+        for b in range(4)
+    ]
+    second_copies = [
+        [
+            pltpu.make_async_remote_copy(
+                src_ref=second_send[b].at[(my_second + d) % 4],
+                dst_ref=second_recv[b].at[d],
+                send_sem=second_ssem.at[b, d],
+                recv_sem=second_rsem.at[b, d],
+                device_id=second_peer(d),
+                device_id_type=MESH,
+            )
+            for d in range(1, 4)
+        ]
+        for b in range(4)
+    ]
 
     def add_core(b):
         core_copies[b].wait_recv()
-        plane_send[b][...] = (
-            core_send[b][sub].astype(jnp.float32) + core_recv[b][...].astype(jnp.float32)
-        ).astype(jnp.bfloat16)
-
-        @pl.loop(1, 16)
-        def _(d):
-            plane_copy(b, d).start()
+        for f in range(4):
+            for g in range(4):
+                at = (f * 4 + g) * (1 - sub) + (g * 4 + f) * sub
+                first_send[b][f, g] = (
+                    core_send[b][sub, at].astype(jnp.float32) + core_recv[b][at].astype(jnp.float32)
+                ).astype(jnp.bfloat16)
+        for copy in first_copies[b]:
+            copy.start()
+
+    def add_first(b):
+        for copy in first_copies[b]:
+            copy.wait_recv()
+        total = first_send[b][my_first].astype(jnp.float32)
+        for d in range(1, 4):
+            total = total + first_recv[b][d].astype(jnp.float32)
+        second_send[b][...] = total.astype(jnp.bfloat16)
+        for copy in second_copies[b]:
+            copy.start()
 
     y_copies = [
         pltpu.make_async_remote_copy(
@@ -180,14 +216,12 @@
         for t in range(3)
     ]
 
-    def add_plane(b):
-        @pl.loop(1, 16)
-        def _(d):
-            plane_copy(b, d).wait_recv()
-
-        total = plane_send[b][z * 4 + x].astype(jnp.float32)
-        for d in range(1, 16):
-            total = total + plane_recv[b][d].astype(jnp.float32)
+    def add_second(b):
+        for copy in second_copies[b]:
+            copy.wait_recv()
+        total = second_send[b][my_second].astype(jnp.float32)
+        for d in range(1, 4):
+            total = total + second_recv[b][d].astype(jnp.float32)
         for u, (t, j) in enumerate(BATCHES[b]):
             column = pl.multiple_of(((y + ORDER[j]) % 4) * TILE, TILE)
             ysum[t, :, pl.ds(column, TILE)] = total[u * 8 : (u + 1) * 8]
@@ -221,7 +255,7 @@
         for j in range(4):
             product(c, 0, j)
 
-    pl.semaphore_wait(barrier, 21)
+    pl.semaphore_wait(barrier, 12)
     boundary = [
         pltpu.make_async_remote_copy(
             src_ref=self_ref.at[local - 1],
@@ -244,13 +278,13 @@
         copy.start()
     pack(0)
     unit_of(1, 1)
+    unit_of(1, 2)
     add_core(0)
-    unit_of(1, 2)
     unit_of(1, 3)
     pack(1)
     unit_of(2, 2)
+    unit_of(2, 3)
     add_core(1)
-    unit_of(2, 3)
     pack(2)
     unit_of(3, 3)
     pack(3)
@@ -266,13 +300,17 @@
 
     cover(0)
     add_core(3)
-    add_plane(0)
+    add_first(0)
     cover(1)
-    add_plane(1)
+    add_first(1)
+    add_second(0)
     cover(2)
-    add_plane(2)
+    add_first(2)
+    add_second(1)
     cover(3)
-    add_plane(3)
+    add_first(3)
+    add_second(2)
+    add_second(3)
     total = ysum[3]
     for t in range(3):
         y_copies[t].wait_recv()
@@ -281,9 +319,8 @@
     for copy in boundary + core_copies + y_copies:
         copy.wait_send()
     for b in range(4):
-        @pl.loop(1, 16)
-        def _(d):
-            plane_copy(b, d).wait_send()
+        for copy in first_copies[b] + second_copies[b]:
+            copy.wait_send()
 
 
 def body(capacity_blocks, capacity_rows, cover_self, cover_prev, scaling):
@@ -295,8 +332,8 @@
     scratch = [pltpu.VMEM((n * per_block + 1, edge, edge), bf16) for n in CHUNKS * 2]
     scratch += [pltpu.VMEM((2, 16, n * 8, TILE), bf16) for n in counts]
     scratch += [pltpu.VMEM((16, n * 8, TILE), bf16) for n in counts]
-    scratch += [pltpu.VMEM((16, n * 8, TILE), bf16) for n in counts]
-    scratch += [pltpu.VMEM((16, n * 8, TILE), bf16) for n in counts]
+    scratch += [pltpu.VMEM((4, 4, n * 8, TILE), bf16) for n in counts * 2]
+    scratch += [pltpu.VMEM((4, n * 8, TILE), bf16) for n in counts * 2]
     scratch += [
         pltpu.VMEM((full, full), f32),
         pltpu.VMEM((local + 8, edge), f32),
@@ -309,7 +346,7 @@
     ]
     scratch += [
         dma((len(CHUNKS),)), dma((2,)), dma((2,)), dma((2,)),
-        dma((4,)), dma((4,)), dma((4, 16)), dma((4, 16)), dma((3,)), dma((3,)),
+        dma((4,)), dma((4,)), dma((4, 4)), dma((4, 4)), dma((4, 4)), dma((4, 4)), dma((3,)), dma((3,)),
     ]
     anywhere = pl.BlockSpec(memory_space=pl.ANY)
     return pl.pallas_call(

time: 41.6 us -> 40.1 us (0.964)
  Pallas kernels: 37.5 us -> 36 us
    pallas_call x1, Pallas kernels: 37.5 us -> 36 us  [body(): pl.pallas_call(functools.partial(kernel, (local, per_block, edge)), out_s...]
where the time goes in v3:
time: 40.1 us; the launch traced here: 39.9 us
  Pallas kernels  36 us (90%)
  local copies, waits for them, and re-layouts  3.25 us (8%)
  between operations  0.64 us (2%)
    pallas_call x1, Pallas kernels, body(): pl.pallas_call(functools.partial(kernel, (local, per_block, edge)), out_s...  36 us
    unnamed x3, local copies, waits for them, and re-layouts  3.25 us

profile of v3, /device:TPU:0, one launch (start us, length us, event | category | flops | bytes accessed | tf_op | source)
XLA Modules:
  0.0 39.9 jit_solution(15518913507177097127)
XLA Ops:
  0.6 36.0 %shard_map.76 = (bf16[64,128,128]{2,1,0:T(8,128)(2,1)S(1)}, bf16[64,128,128]{2,1,0:T(8,128)(2,1)S(1)}, f32[8,1024]{1,0:T(8,128)S(1)}) custom-call(bf16[320,128,128]{2,1,0:T(8,128)(2,1)} %bitcast.2, s32[5,64]{1,0:T(8,128)} %bitcast.3, bf16[64,128,128]{2,1,0:T(8,128)(2,1)} %self_ref.1, bf16[64,128,128]{2,1,0:T(8,128)(2,1)} %prev_ref.1, bf16[64,128]{1,0:T(8,128)(2,1)} %scal_ref.1), custom_call_target="tpu_custom_call" | custom-call | tf_op jit(solution)/shard_map/pallas_call | solution.py:352
  36.6 1.3 %copy.11 = bf16[64,128,128]{2,1,0:T(8,128)(2,1)} copy(bf16[64,128,128]{2,1,0:T(8,128)(2,1)S(1)} %get-tuple-element.3) | data formatting | bytes 4194304
  37.9 0.6 %copy.13 = f32[8,1024]{1,0:T(8,128)} copy(f32[8,1024]{1,0:T(8,128)S(1)} %get-tuple-element.5) | data formatting | bytes 65536
  38.5 1.3 %copy.12 = bf16[64,128,128]{2,1,0:T(8,128)(2,1)} copy(bf16[64,128,128]{2,1,0:T(8,128)(2,1)S(1)} %get-tuple-element.4) | data formatting | bytes 4194304

commit v4 on v3

--- a/solution.py
+++ b/solution.py
@@ -287,8 +287,8 @@
     add_core(1)
     pack(2)
     unit_of(3, 3)
+    add_core(2)
     pack(3)
-    add_core(2)
 
     for copy in cover_loads:
         copy.wait()
@@ -323,6 +323,15 @@
             copy.wait_send()
 
 
+def write_out(*refs):
+    held, outs, sem = refs[:3], refs[3:6], refs[6]
+    copies = [pltpu.make_async_copy(held[i], outs[i], sem.at[i]) for i in range(3)]
+    for copy in copies:
+        copy.start()
+    for copy in copies:
+        copy.wait()
+
+
 def body(capacity_blocks, capacity_rows, cover_self, cover_prev, scaling):
     local, per_block, edge, _ = capacity_blocks.shape
     full = CAP * edge
@@ -349,7 +358,7 @@
         dma((4,)), dma((4,)), dma((4, 4)), dma((4, 4)), dma((4, 4)), dma((4, 4)), dma((3,)), dma((3,)),
     ]
     anywhere = pl.BlockSpec(memory_space=pl.ANY)
-    return pl.pallas_call(
+    held = pl.pallas_call(
         functools.partial(kernel, (local, per_block, edge)),
         out_shape=(
             pltpu.VMEM((local, edge, edge), bf16),
@@ -369,6 +378,14 @@
             collective_id=0, has_side_effects=True, vmem_limit_bytes=50 << 20
         ),
     )(capacity_blocks.reshape(local * per_block, edge, edge), capacity_rows.T, cover_self, cover_prev, scaling)
+    return pl.pallas_call(
+        write_out,
+        out_shape=tuple(jax.ShapeDtypeStruct(value.shape, value.dtype) for value in held),
+        in_specs=[pl.BlockSpec(memory_space=pltpu.VMEM)] * 3,
+        out_specs=(anywhere,) * 3,
+        scratch_shapes=[dma((3,))],
+        compiler_params=pltpu.CompilerParams(vmem_limit_bytes=1 << 20),
+    )(*held)
 
 
 def solution(mesh):

time: 40.1 us -> 38.9 us (0.970)
  local copies, waits for them, and re-layouts: 3.25 us -> 0 us
  Pallas kernels: 36 us -> 37.9 us
    unnamed x3 -> x0, local copies, waits for them, and re-layouts: 3.25 us -> none
    pallas_call x0 -> x1, Pallas kernels: none -> 2.04 us  [body(): pl.pallas_call(write_out, out_shape=tuple((jax.ShapeDtypeStruct(value.sha...]
where the time goes in v4:
time: 38.9 us; the launch traced here: 38.7 us
  Pallas kernels  37.9 us (97%)
  between operations  0.8 us (2%)
    pallas_call x1, Pallas kernels, body(): pl.pallas_call(functools.partial(kernel, (local, per_block, edge)), out_s...  35.9 us
    pallas_call x1, Pallas kernels, body(): pl.pallas_call(write_out, out_shape=tuple((jax.ShapeDtypeStruct(value.sha...  2.04 us

profile of v4, /device:TPU:0, one launch (start us, length us, event | category | flops | bytes accessed | tf_op | source)
XLA Modules:
  0.0 38.7 jit_solution(10611730966019701352)
XLA Ops:
  0.6 35.9 %shard_map.76 = (bf16[64,128,128]{2,1,0:T(8,128)(2,1)S(1)}, bf16[64,128,128]{2,1,0:T(8,128)(2,1)S(1)}, f32[8,1024]{1,0:T(8,128)S(1)}) custom-call(bf16[320,128,128]{2,1,0:T(8,128)(2,1)} %bitcast.2, s32[5,64]{1,0:T(8,128)} %bitcast.3, bf16[64,128,128]{2,1,0:T(8,128)(2,1)} %self_ref.1, bf16[64,128,128]{2,1,0:T(8,128)(2,1)} %prev_ref.1, bf16[64,128]{1,0:T(8,128)(2,1)} %scal_ref.1), custom_call_target="tpu_custom_call" | custom-call | tf_op jit(solution)/shard_map/pallas_call | solution.py:361
  36.5 2.0 %shard_map.77 = (bf16[64,128,128]{2,1,0:T(8,128)(2,1)}, bf16[64,128,128]{2,1,0:T(8,128)(2,1)}, f32[8,1024]{1,0:T(8,128)}) custom-call(bf16[64,128,128]{2,1,0:T(8,128)(2,1)S(1)} %get-tuple-element.6.refs_0_, bf16[64,128,128]{2,1,0:T(8,128)(2,1)S(1)} %get-tuple-element.7.refs_1_, f32[8,1024]{1,0:T(8,128)S(1)} %get-tuple-element.8.refs_2_), custom_call_target="tpu_custom_call" | custom-call | tf_op jit(solution)/shard_map/pallas_call | solution.py:381

commit v5 on v4

--- a/solution.py
+++ b/solution.py
@@ -301,15 +301,15 @@
     cover(0)
     add_core(3)
     add_first(0)
+    add_first(1)
     cover(1)
-    add_first(1)
     add_second(0)
+    add_first(2)
+    add_first(3)
     cover(2)
-    add_first(2)
     add_second(1)
+    add_second(2)
     cover(3)
-    add_first(3)
-    add_second(2)
     add_second(3)
     total = ysum[3]
     for t in range(3):

time: 38.9 us -> 39 us (level)
  no operation moved by 1% of the time
where the time goes in v5:
time: 39 us; the launch traced here: 38.8 us
  Pallas kernels  38 us (97%)
  between operations  0.8 us (2%)
    pallas_call x1, Pallas kernels, body(): pl.pallas_call(functools.partial(kernel, (local, per_block, edge)), out_s...  36 us
    pallas_call x1, Pallas kernels, body(): pl.pallas_call(write_out, out_shape=tuple((jax.ShapeDtypeStruct(value.sha...  2.04 us

profile of v5, /device:TPU:0, one launch (start us, length us, event | category | flops | bytes accessed | tf_op | source)
XLA Modules:
  0.0 38.8 jit_solution(14250400373598943852)
XLA Ops:
  0.6 36.0 %shard_map.76 = (bf16[64,128,128]{2,1,0:T(8,128)(2,1)S(1)}, bf16[64,128,128]{2,1,0:T(8,128)(2,1)S(1)}, f32[8,1024]{1,0:T(8,128)S(1)}) custom-call(bf16[320,128,128]{2,1,0:T(8,128)(2,1)} %bitcast.2, s32[5,64]{1,0:T(8,128)} %bitcast.3, bf16[64,128,128]{2,1,0:T(8,128)(2,1)} %self_ref.1, bf16[64,128,128]{2,1,0:T(8,128)(2,1)} %prev_ref.1, bf16[64,128]{1,0:T(8,128)(2,1)} %scal_ref.1), custom_call_target="tpu_custom_call" | custom-call | tf_op jit(solution)/shard_map/pallas_call | solution.py:361
  36.6 2.0 %shard_map.77 = (bf16[64,128,128]{2,1,0:T(8,128)(2,1)}, bf16[64,128,128]{2,1,0:T(8,128)(2,1)}, f32[8,1024]{1,0:T(8,128)}) custom-call(bf16[64,128,128]{2,1,0:T(8,128)(2,1)S(1)} %get-tuple-element.6.refs_0_, bf16[64,128,128]{2,1,0:T(8,128)(2,1)S(1)} %get-tuple-element.7.refs_1_, f32[8,1024]{1,0:T(8,128)S(1)} %get-tuple-element.8.refs_2_), custom_call_target="tpu_custom_call" | custom-call | tf_op jit(solution)/shard_map/pallas_call | solution.py:381
